TPU v7x, 512 devices: a whole 4x8x8 slice. The times are simulated.
512 devices in a mesh: row: 8 (over y), col: 64 (over z, x, core).
Axes of the slice: x: 4, y: 8, z: 8, core: 2. Of those that a mesh axis runs over, the one named last changes fastest.
Arguments:
- ppmi: bfloat16 [4096, 128256], P('row', 'col'), may hold values from -12000 to 12000
- basis: bfloat16 [256, 128256], P(None, 'col'), may hold values from -10 to 10
Outputs:
- left_basis: bfloat16 [256, 4096], P(None, 'row')
- right_basis: bfloat16 [256, 128256], P(None, 'col')
All inputs are finite; a program needn't handle non-finite values.
Results may differ from a plain program's by a relative error of at most 0.0045.
Values may be sent and summed in bfloat16 or wider, within the bound.
A program may use at most 128 MiB of HBM per device.

v0:
```python
import jax
import jax.numpy as jnp
from jax import lax
from jax.sharding import Mesh
from jax.sharding import PartitionSpec as P

COL = ("col_0", "col_1", "col_2")


def in_blocks(array, dim, peers):
    before, after = (array.shape[:dim], array.shape[dim + 1 :])
    return jnp.moveaxis(array.reshape(*before, peers, -1, *after), dim, 0)


def sum_at_owner(array, axis, dim):
    peers = lax.axis_size(axis)
    pieces = lax.all_to_all(in_blocks(array, dim, peers), axis, 0, 0, tiled=True)
    return jnp.sum(pieces, axis=0)


def summed_rows(array, axes, dim):
    far, near = axes
    pieces = in_blocks(array, dim, lax.axis_size(far))
    nearer = sum_at_owner(pieces, near, dim + 1)
    arrived = lax.all_to_all(nearer, far, split_axis=0, concat_axis=0, tiled=True)
    return arrived.sum(axis=0)


def rows_for(lines, peers):
    spare = -len(lines) % peers
    return jnp.pad(lines, [(0, spare)] + [(0, 0)] * (lines.ndim - 1))


def copy_for_each(array, axis):
    peers = lax.axis_size(axis)
    return lax.all_to_all(
        jnp.broadcast_to(array[None], (peers, *array.shape)), axis, 0, 0, tiled=True
    )


def joined_along(pieces, dim):
    shape = list(pieces.shape[1:])
    shape[dim] *= pieces.shape[0]
    return jnp.moveaxis(pieces, 0, dim).reshape(shape)


def gathered_by_axis(array, axes, dim):
    far, near = axes
    pieces = copy_for_each(copy_for_each(array, far), near)
    return joined_along(pieces.swapaxes(0, 1).reshape(-1, *array.shape), dim)


def nested_sum(array, axes):
    lines = array.reshape(-1, array.shape[-1])
    own = summed_rows(rows_for(lines, lax.axis_size(axes[0]) * lax.axis_size(axes[1])), axes, 0)
    whole = gathered_by_axis(own, axes, 0)
    return whole[: len(lines)].reshape(array.shape)


def of_everyone(array, axis):
    everything = copy_for_each(array, axis)
    return jnp.sum(everything, axis=0)


def local_gram(block):
    return jnp.dot(block, block.T, precision=lax.Precision.HIGHEST)


def solve_rows(gram, block):
    lower = jnp.linalg.cholesky(gram)
    solved = lax.linalg.triangular_solve(lower, block, left_side=True, lower=True)
    return solved.astype(jnp.bfloat16)


def local(ppmi, basis):
    rows_total = ppmi.shape[0] * lax.axis_size("row")
    cols_total = ppmi.shape[1] * lax.axis_size(COL)
    basis_now = basis
    left = None
    partial_value = lax.dot_general(
        basis_now, ppmi, (((1,), (1,)), ((), ())), preferred_element_type=jnp.float32
    )
    y_total = nested_sum(partial_value, (("col_0", "col_1"), "col_2"))
    gram_left = of_everyone(local_gram(y_total), "row") / rows_total
    left = solve_rows(gram_left, y_total)
    z_part = jnp.dot(left, ppmi, preferred_element_type=jnp.float32)
    z_total = lax.psum(z_part, "row")
    gram_right = nested_sum(local_gram(z_total), (("col_0", "col_1"), "col_2")) / cols_total
    basis_now = solve_rows(gram_right, z_total)
    return (left, basis_now)


def solution(mesh):
    split = Mesh(
        mesh.devices.reshape(mesh.shape["row"], 8, 4, 2), ("row", "col_0", "col_1", "col_2")
    )
    placed = (P("row", COL), P(None, COL))
    return jax.shard_map(
        local,
        mesh=split,
        in_specs=placed,
        out_specs=(P(None, "row"), P(None, COL)),
        check_vma=False,
    )
```

profile of v0, /device:TPU:1, one launch (start us, length us, event | category | flops | bytes accessed | tf_op | source)
XLA Modules:
  0.0 395.1 jit_solution(5545338627759966449)
XLA Ops:
  7.2 1.6 copy-done
  8.7 1.9 fusion.18
  10.8 0.8 copy.40
  11.7 10.4 %all-to-all-start = ((f32[2,32,4,512]{3,2,1,0:T(4,128)}), f32[2,32,4,512]{3,2,1,0:T(4,128)S(1)}, u32[]{:S(2)}, u32[]{:S(2)}) async-start(f32[2,32,4,512]{3,2,1,0:T(4,128)} %bitcast.70), calls=%async_computation | async-start | bytes 1048576 | tf_op jit(solution)/shard_map/all_to_all | solution.py:17
  22.0 1.4 all-to-all-done
  23.6 18.9 %all_to_all.49 = f32[32,4,512]{2,1,0:T(4,128)S(1)} all-to-all(f32[32,4,512]{2,1,0:T(4,128)S(1)} %reduce_sum.45), channel_id=1, replica_groups=mesh['row'=8,'col_0'=8,'col_1'=4,'col_2'=2] {'col_0','col_1'}, dimensions={0} | all-to-all | bytes 524288 | tf_op jit(solution)/shard_map/all_to_all | solution.py:25
  42.6 15.0 %all_to_all.45 = f32[32,4,512]{2,1,0:T(4,128)S(1)} all-to-all(f32[32,4,512]{2,1,0:T(4,128)S(1)} %broadcast_in_dim.10), channel_id=1, replica_groups=mesh['row'=8,'col_0'=8,'col_1'=4,'col_2'=2] {'col_0','col_1'}, dimensions={0} | all-to-all | bytes 524288 | tf_op jit(solution)/shard_map/all_to_all | solution.py:36
  57.7 7.1 %all_to_all.46 = f32[2,32,4,512]{3,2,1,0:T(4,128)S(1)} all-to-all(f32[2,32,4,512]{3,2,1,0:T(4,128)S(1)} %broadcast_in_dim.11), channel_id=1, replica_groups=mesh['row'=8,'col_0'=8,'col_1'=4,'col_2'=2] {'col_2'}, dimensions={0} | all-to-all | bytes 1048576 | tf_op jit(solution)/shard_map/all_to_all | solution.py:36
  64.7 0.9 copy.27
  65.6 1.2 reshape_reshape.11
  66.8 0.6 fusion.19
  67.5 1.5 broadcast_in_dim.12
  68.9 6.8 %all-to-all-start.4 = ((f32[8,256,256]{2,1,0:T(8,128)}), f32[8,256,256]{2,1,0:T(8,128)}, u32[]{:S(2)}, u32[]{:S(2)}) async-start(f32[8,256,256]{2,1,0:T(8,128)} %broadcast_in_dim.12), calls=%async_computation.4 | async-start | bytes 4194304 | tf_op jit(solution)/shard_map/all_to_all | solution.py:36
  76.4 47.8 %all-to-all-done.4 = f32[8,256,256]{2,1,0:T(8,128)} async-done(((f32[8,256,256]{2,1,0:T(8,128)}), f32[8,256,256]{2,1,0:T(8,128)}, u32[]{:S(2)}, u32[]{:S(2)}) %all-to-all-start.4) | async-done | bytes 2097184 | tf_op jit(solution)/shard_map/all_to_all | solution.py:36
  124.2 1.8 reduce_sum.47
  126.3 11.7 %cholesky.130 = f32[128,128]{1,0:T(8,128)S(1)} custom-call(f32[128,128]{1,0:T(8,128)S(1)} %cholesky.194), custom_call_target="Cholesky" | custom-call | tf_op jit(solution)/shard_map/jit(cholesky)/cholesky | solution.py:70
  138.1 9.8 %custom-call.17 = f32[1,128,128]{1,2,0:T(8,128)S(1)} custom-call(f32[1,128,128]{2,1,0:T(8,128)S(1)} %get-tuple-element.48), custom_call_target="InvertDiagBlocksLowerTriangular" | custom-call | tf_op jit(solution)/shard_map/jit(cholesky)/cholesky | solution.py:70
  148.4 11.7 %cholesky.147 = f32[128,128]{1,0:T(8,128)S(1)} custom-call(f32[128,128]{1,0:T(8,128)S(1)} %convolution_subtract_fusion.3), custom_call_target="Cholesky" | custom-call | tf_op jit(solution)/shard_map/jit(cholesky)/cholesky | solution.py:70
  160.1 0.7 compare_reduce_fusion.2
  162.2 4.6 %while.2 = (s32[]{:T(128)}, f32[256,256]{1,0:T(8,128)S(1)}, s32[2,2]{1,0:T(2,128)S(1)}, f32[2,128,128]{2,1,0:T(8,128)S(1)}, s32[]{:T(128)}) while((s32[]{:T(128)}, f32[256,256]{1,0:T(8,128)S(1)}, s32[2,2]{1,0:T(2,128)S(1)}, f32[2,128,128]{2,1,0:T(8,128)S(1)}, s32[]{:T(128)}) %tuple.48), condition=%wide.while_cond, body=%wide.while_body.sunk | while | flops 2 | bytes 131189 | solution.py:71
  162.8 0.7 fusion.41
  163.5 1.3 bitcast_dynamic-update-slice_fusion.4
  164.8 0.7 fusion.41
  165.5 1.3 bitcast_dynamic-update-slice_fusion.4
  166.8 19.7 %custom-call.14 = f32[2,128,128]{1,2,0:T(8,128)S(1)} custom-call(f32[2,128,128]{2,1,0:T(8,128)S(1)} %get-tuple-element.10), custom_call_target="InvertDiagBlocksLowerTriangular" | custom-call | tf_op jit(solution)/shard_map/triangular_solve | solution.py:71
  187.3 0.4 convolution_convert_fusion.1
  187.8 2.0 fusion.20
  189.8 77.2 %all-reduce.3.cloned.1.call-done = f32[256,2004]{0,1:T(8,128)} async-done(((f32[256,2004]{0,1:T(8,128)}), f32[256,2004]{0,1:T(8,128)}) %all-reduce.3.cloned.1.call-update) | async-done | bytes 2052112 | tf_op jit(solution)/shard_map/psum | solution.py:87
  267.0 5.7 %fusion.21 = f32[256,256]{1,0:T(8,128)S(1)} fusion(f32[256,2004]{0,1:T(8,128)} %all-reduce.3.cloned.1.call-done), kind=kOutput, calls=%fused_computation.63 | convolution fusion | flops 1576009728 | bytes 2314240 | tf_op jit(solution)/shard_map/dot_general | solution.py:66
  272.8 7.7 %all_to_all.47 = f32[2,32,4,256]{3,2,1,0:T(4,128)S(1)} all-to-all(f32[2,32,4,256]{3,2,1,0:T(4,128)S(1)} %bitcast.86), channel_id=1, replica_groups=mesh['row'=8,'col_0'=8,'col_1'=4,'col_2'=2] {'col_2'}, dimensions={0} | all-to-all | bytes 524288 | tf_op jit(solution)/shard_map/all_to_all | solution.py:17
  280.5 19.1 %all_to_all.50 = f32[32,4,256]{2,1,0:T(4,128)S(1)} all-to-all(f32[32,4,256]{2,1,0:T(4,128)S(1)} %reduce_sum.48), channel_id=1, replica_groups=mesh['row'=8,'col_0'=8,'col_1'=4,'col_2'=2] {'col_0','col_1'}, dimensions={0} | all-to-all | bytes 262144 | tf_op jit(solution)/shard_map/all_to_all | solution.py:25
  299.7 13.0 %all_to_all.51 = f32[32,4,256]{2,1,0:T(4,128)S(1)} all-to-all(f32[32,4,256]{2,1,0:T(4,128)S(1)} %broadcast_in_dim.14), channel_id=1, replica_groups=mesh['row'=8,'col_0'=8,'col_1'=4,'col_2'=2] {'col_0','col_1'}, dimensions={0} | all-to-all | bytes 262144 | tf_op jit(solution)/shard_map/all_to_all | solution.py:36
  312.7 6.6 %all_to_all.48 = f32[2,32,4,256]{3,2,1,0:T(4,128)S(1)} all-to-all(f32[2,32,4,256]{3,2,1,0:T(4,128)S(1)} %broadcast_in_dim.15), channel_id=1, replica_groups=mesh['row'=8,'col_0'=8,'col_1'=4,'col_2'=2] {'col_2'}, dimensions={0} | all-to-all | bytes 524288 | tf_op jit(solution)/shard_map/all_to_all | solution.py:36
  319.8 11.7 %cholesky.164 = f32[128,128]{1,0:T(8,128)S(1)} custom-call(f32[128,128]{1,0:T(8,128)S(1)} %cholesky.197), custom_call_target="Cholesky" | custom-call | tf_op jit(solution)/shard_map/jit(cholesky)/cholesky | solution.py:70
  331.5 0.7 compare_reduce_fusion.1
  332.2 9.8 %custom-call.18 = f32[1,128,128]{1,2,0:T(8,128)S(1)} custom-call(f32[1,128,128]{2,1,0:T(8,128)S(1)} %get-tuple-element.44), custom_call_target="InvertDiagBlocksLowerTriangular" | custom-call | tf_op jit(solution)/shard_map/jit(cholesky)/cholesky | solution.py:70
  342.5 11.7 %cholesky.181 = f32[128,128]{1,0:T(8,128)S(1)} custom-call(f32[128,128]{1,0:T(8,128)S(1)} %convolution_subtract_fusion.2), custom_call_target="Cholesky" | custom-call | tf_op jit(solution)/shard_map/jit(cholesky)/cholesky | solution.py:70
  354.3 0.6 compare_reduce_fusion
  356.2 4.1 %while.3 = (s32[]{:T(128)}, f32[256,256]{1,0:T(8,128)S(1)}, s32[2,2]{1,0:T(2,128)S(1)}, f32[2,128,128]{2,1,0:T(8,128)S(1)}, s32[]{:T(128)}) while((s32[]{:T(128)}, f32[256,256]{1,0:T(8,128)S(1)}, s32[2,2]{1,0:T(2,128)S(1)}, f32[2,128,128]{2,1,0:T(8,128)S(1)}, s32[]{:T(128)}) %tuple.56), condition=%wide.while_cond.1, body=%wide.while_body.1.sunk | while | flops 2 | bytes 131189 | solution.py:71
  356.3 0.7 fusion.42
  356.9 1.3 bitcast_dynamic-update-slice_fusion.5
  358.3 0.7 fusion.42
  359.0 1.3 bitcast_dynamic-update-slice_fusion.5
  360.3 19.9 %custom-call.15 = f32[2,128,128]{1,2,0:T(8,128)S(1)} custom-call(f32[2,128,128]{2,1,0:T(8,128)S(1)} %get-tuple-element.18), custom_call_target="InvertDiagBlocksLowerTriangular" | custom-call | tf_op jit(solution)/shard_map/triangular_solve | solution.py:71
  380.2 3.1 fusion.17
  383.4 1.8 convolution_subtract_fusion
  385.2 1.7 convolution_convert_fusion
  386.9 1.1 pad_maximum_fusion
  (57 shorter events, 4.2 us)
Async XLA Ops:
  7.2 1.6 copy-start
  11.7 11.7 %all-to-all-start = ((f32[2,32,4,512]{3,2,1,0:T(4,128)}), f32[2,32,4,512]{3,2,1,0:T(4,128)S(1)}, u32[]{:S(2)}, u32[]{:S(2)}) async-start(f32[2,32,4,512]{3,2,1,0:T(4,128)} %bitcast.70), calls=%async_computation | async-start | bytes 1048576 | tf_op jit(solution)/shard_map/all_to_all | solution.py:17
  68.9 55.3 %all-to-all-start.4 = ((f32[8,256,256]{2,1,0:T(8,128)}), f32[8,256,256]{2,1,0:T(8,128)}, u32[]{:S(2)}, u32[]{:S(2)}) async-start(f32[8,256,256]{2,1,0:T(8,128)} %broadcast_in_dim.12), calls=%async_computation.4 | async-start | bytes 4194304 | tf_op jit(solution)/shard_map/all_to_all | solution.py:36
  75.8 191.3 %all-reduce.3.cloned.1.call-start = ((), (), s32[]{:S(2)}) async-start(), calls=%async_computation.9 | async-start | bytes 4112384 | tf_op jit(solution)/shard_map/psum | solution.py:87
  187.8 2.0 copy-start.2
  380.2 3.1 copy-start.1
Sparse Core Ops, SparseCore 0:
  190.0 77.0 all-reduce.2
where the time goes:
time: 399 us; the launch traced here: 395 us
  waiting for transfers between devices  126 us (32%)
  other arithmetic  112 us (28%)
  blocking collectives  87.3 us (22%)
  matrix products  19.1 us (5%)
  starting transfers between devices  17.5 us (4%)
  between operations  17.2 us (4%)
  local copies, waits for them, and re-layouts  15.3 us (4%)
    psum x1, waiting for transfers between devices, local(): z_total = lax.psum(z_part, 'row')  77.2 us
    another operation x13, other arithmetic, solve_rows(): lower = jnp.linalg.cholesky(gram)  68.7 us
    all_to_all x1, waiting for transfers between devices, copy_for_each(): lax.all_to_all(jnp.broadcast_to(array[None], (peers, *array.shape)), axis...  47.8 us
    all_to_all x4, blocking collectives, copy_for_each(): lax.all_to_all(jnp.broadcast_to(array[None], (peers, *array.shape)), axis...  41.7 us
    another operation x7, other arithmetic, solve_rows(): lax.linalg.triangular_solve(lower, block, left_side=True, lower=True)  40.7 us
    all_to_all x2, blocking collectives, summed_rows(): lax.all_to_all(nearer, far, split_axis=0, concat_axis=0, tiled=True)  37.9 us
    all_to_all x1, starting transfers between devices, sum_at_owner(): lax.all_to_all(in_blocks(array, dim, peers), axis, 0, 0, tiled=True)  10.4 us
    another operation x12, local copies, waits for them, and re-layouts  8.04 us
  transfers between devices with their start and end apart: 3, of which 3 were waited for; matrix products, arithmetic and copies ran while one was open for 0% of the time, Pallas kernels for 0%

commit v1 on v0

--- a/solution.py
+++ b/solution.py
@@ -84,7 +84,7 @@
     gram_left = of_everyone(local_gram(y_total), "row") / rows_total
     left = solve_rows(gram_left, y_total)
     z_part = jnp.dot(left, ppmi, preferred_element_type=jnp.float32)
-    z_total = lax.psum(z_part, "row")
+    z_total = jnp.sum(lax.all_gather(z_part, "row"), axis=0)
     gram_right = nested_sum(local_gram(z_total), (("col_0", "col_1"), "col_2")) / cols_total
     basis_now = solve_rows(gram_right, z_total)
     return (left, basis_now)

time: 399 us -> 507 us (1.27)
  waiting for transfers between devices: 126 us -> 214 us
  local copies, waits for them, and re-layouts: 15.3 us -> 31 us
  other arithmetic: 112 us -> 120 us
    all_gather x0 -> x1, waiting for transfers between devices: none -> 165 us  [local(): z_total = jnp.sum(lax.all_gather(z_part, 'row'), axis=0)]
    psum x1 -> x0, waiting for transfers between devices: 77.2 us -> none  [local(): z_total = lax.psum(z_part, 'row')]
    unnamed x8 -> x11, local copies, waits for them, and re-layouts: 1.61 us -> 12.5 us
    reduce_sum x0 -> x1, other arithmetic: none -> 8.61 us  [local(): z_total = jnp.sum(lax.all_gather(z_part, 'row'), axis=0)]
where the time goes in v1:
time: 507 us; the launch traced here: 503 us
  waiting for transfers between devices  214 us (42%)
  other arithmetic  120 us (24%)
  blocking collectives  84 us (17%)
  local copies, waits for them, and re-layouts  31 us (6%)
  matrix products  18 us (4%)
  starting transfers between devices  17.7 us (3%)
  between operations  17.2 us (3%)
    all_gather x1, waiting for transfers between devices, local(): z_total = jnp.sum(lax.all_gather(z_part, 'row'), axis=0)  165 us
    another operation x13, other arithmetic, solve_rows(): lower = jnp.linalg.cholesky(gram)  68.7 us
    all_to_all x1, waiting for transfers between devices, copy_for_each(): lax.all_to_all(jnp.broadcast_to(array[None], (peers, *array.shape)), axis...  47.6 us
    all_to_all x4, blocking collectives, copy_for_each(): lax.all_to_all(jnp.broadcast_to(array[None], (peers, *array.shape)), axis...  41.8 us
    another operation x7, other arithmetic, solve_rows(): lax.linalg.triangular_solve(lower, block, left_side=True, lower=True)  40.8 us
    all_to_all x2, blocking collectives, summed_rows(): lax.all_to_all(nearer, far, split_axis=0, concat_axis=0, tiled=True)  37.9 us
    unnamed x11, local copies, waits for them, and re-layouts  12.5 us
    all_to_all x1, starting transfers between devices, sum_at_owner(): lax.all_to_all(in_blocks(array, dim, peers), axis, 0, 0, tiled=True)  10.4 us
  transfers between devices with their start and end apart: 3, of which 3 were waited for; matrix products, arithmetic and copies ran while one was open for 0% of the time, Pallas kernels for 0%

profile of v1, /device:TPU:1, one launch (start us, length us, event | category | flops | bytes accessed | tf_op | source)
XLA Modules:
  0.0 502.8 jit_solution(8747175505193674600)
XLA Ops:
  7.2 1.6 copy-done
  8.7 1.9 fusion.26
  10.8 0.8 copy.60
  11.7 10.4 %all-to-all-start = ((f32[2,32,4,512]{3,2,1,0:T(4,128)}), f32[2,32,4,512]{3,2,1,0:T(4,128)S(1)}, u32[]{:S(2)}, u32[]{:S(2)}) async-start(f32[2,32,4,512]{3,2,1,0:T(4,128)} %bitcast.81), calls=%async_computation | async-start | bytes 1048576 | tf_op jit(solution)/shard_map/all_to_all | solution.py:17
  22.0 1.4 all-to-all-done
  23.6 18.9 %all_to_all.49 = f32[32,4,512]{2,1,0:T(4,128)S(1)} all-to-all(f32[32,4,512]{2,1,0:T(4,128)S(1)} %reduce_sum.54), channel_id=1, replica_groups=mesh['row'=8,'col_0'=8,'col_1'=4,'col_2'=2] {'col_0','col_1'}, dimensions={0} | all-to-all | bytes 524288 | tf_op jit(solution)/shard_map/all_to_all | solution.py:25
  42.6 15.0 %all_to_all.45 = f32[32,4,512]{2,1,0:T(4,128)S(1)} all-to-all(f32[32,4,512]{2,1,0:T(4,128)S(1)} %broadcast_in_dim.10), channel_id=1, replica_groups=mesh['row'=8,'col_0'=8,'col_1'=4,'col_2'=2] {'col_0','col_1'}, dimensions={0} | all-to-all | bytes 524288 | tf_op jit(solution)/shard_map/all_to_all | solution.py:36
  57.7 7.1 %all_to_all.46 = f32[2,32,4,512]{3,2,1,0:T(4,128)S(1)} all-to-all(f32[2,32,4,512]{3,2,1,0:T(4,128)S(1)} %broadcast_in_dim.11), channel_id=1, replica_groups=mesh['row'=8,'col_0'=8,'col_1'=4,'col_2'=2] {'col_2'}, dimensions={0} | all-to-all | bytes 1048576 | tf_op jit(solution)/shard_map/all_to_all | solution.py:36
  64.7 0.9 copy.42
  65.6 1.2 reshape_reshape.9
  67.5 1.5 broadcast_in_dim.12
  68.9 6.8 %all-to-all-start.4 = ((f32[8,256,256]{2,1,0:T(8,128)}), f32[8,256,256]{2,1,0:T(8,128)}, u32[]{:S(2)}, u32[]{:S(2)}) async-start(f32[8,256,256]{2,1,0:T(8,128)} %broadcast_in_dim.12), calls=%async_computation.4 | async-start | bytes 4194304 | tf_op jit(solution)/shard_map/all_to_all | solution.py:36
  76.6 47.6 %all-to-all-done.4 = f32[8,256,256]{2,1,0:T(8,128)} async-done(((f32[8,256,256]{2,1,0:T(8,128)}), f32[8,256,256]{2,1,0:T(8,128)}, u32[]{:S(2)}, u32[]{:S(2)}) %all-to-all-start.4) | async-done | bytes 2097184 | tf_op jit(solution)/shard_map/all_to_all | solution.py:36
  124.2 1.8 reduce_sum.56
  126.3 11.7 %cholesky.130 = f32[128,128]{1,0:T(8,128)S(1)} custom-call(f32[128,128]{1,0:T(8,128)S(1)} %cholesky.194), custom_call_target="Cholesky" | custom-call | tf_op jit(solution)/shard_map/jit(cholesky)/cholesky | solution.py:70
  138.1 9.8 %custom-call.17 = f32[1,128,128]{1,2,0:T(8,128)S(1)} custom-call(f32[1,128,128]{2,1,0:T(8,128)S(1)} %get-tuple-element.48), custom_call_target="InvertDiagBlocksLowerTriangular" | custom-call | tf_op jit(solution)/shard_map/jit(cholesky)/cholesky | solution.py:70
  148.4 11.7 %cholesky.147 = f32[128,128]{1,0:T(8,128)S(1)} custom-call(f32[128,128]{1,0:T(8,128)S(1)} %convolution_subtract_fusion.3), custom_call_target="Cholesky" | custom-call | tf_op jit(solution)/shard_map/jit(cholesky)/cholesky | solution.py:70
  160.1 0.7 compare_reduce_fusion.2
  162.2 4.2 while.2
  162.4 0.7 fusion.46
  163.1 1.3 bitcast_dynamic-update-slice_fusion.4
  164.5 0.7 fusion.46
  165.1 1.3 bitcast_dynamic-update-slice_fusion.4
  166.5 19.7 %custom-call.14 = f32[2,128,128]{1,2,0:T(8,128)S(1)} custom-call(f32[2,128,128]{2,1,0:T(8,128)S(1)} %get-tuple-element.10), custom_call_target="InvertDiagBlocksLowerTriangular" | custom-call | tf_op jit(solution)/shard_map/triangular_solve | solution.py:71
  187.4 2.0 fusion.28
  189.5 165.4 %all-gather.3.cloned.1.call-done = f32[2048,2004]{0,1:T(8,128)} async-done(((f32[256,2004]{0,1:T(8,128)}), f32[2048,2004]{0,1:T(8,128)}) %all-gather.3.cloned.1.call-update) | async-done | bytes 16416784 | tf_op jit(solution)/shard_map/all_gather | solution.py:87
  354.9 10.9 %copy.54 = f32[251,8,8,256]{3,2,1,0:T(8,128)S(1)} copy(f32[251,8,8,256]{3,1,2,0:T(8,128)} %bitcast.95) | data formatting | bytes 32899072
  365.8 8.6 %bitcast_reduce_fusion = f32[256,2004]{0,1:T(8,128)S(1)} fusion(f32[2008,8,256]{2,1,0:T(8,128)S(1)} %bitcast.94), kind=kLoop, calls=%fused_computation.4 | loop fusion | flops 3591168 | bytes 18468864 | tf_op jit(solution)/shard_map/reduce_sum | solution.py:87
  374.4 2.0 copy.47
  376.4 2.9 dot_general.17
  379.2 4.6 fusion.3
  383.8 4.3 all_to_all.47
  388.2 19.1 %all_to_all.50 = f32[32,4,256]{2,1,0:T(4,128)S(1)} all-to-all(f32[32,4,256]{2,1,0:T(4,128)S(1)} %copy.49), channel_id=1, replica_groups=mesh['row'=8,'col_0'=8,'col_1'=4,'col_2'=2] {'col_0','col_1'}, dimensions={0} | all-to-all | bytes 262144 | tf_op jit(solution)/shard_map/all_to_all | solution.py:25
  407.3 13.0 %all_to_all.51 = f32[32,4,256]{2,1,0:T(4,128)S(1)} all-to-all(f32[32,4,256]{2,1,0:T(4,128)S(1)} %broadcast_in_dim.14), channel_id=1, replica_groups=mesh['row'=8,'col_0'=8,'col_1'=4,'col_2'=2] {'col_0','col_1'}, dimensions={0} | all-to-all | bytes 262144 | tf_op jit(solution)/shard_map/all_to_all | solution.py:36
  420.4 6.7 %all_to_all.48 = f32[2,32,4,256]{3,2,1,0:T(4,128)S(1)} all-to-all(f32[2,32,4,256]{3,2,1,0:T(4,128)S(1)} %broadcast_in_dim.15), channel_id=1, replica_groups=mesh['row'=8,'col_0'=8,'col_1'=4,'col_2'=2] {'col_2'}, dimensions={0} | all-to-all | bytes 524288 | tf_op jit(solution)/shard_map/all_to_all | solution.py:36
  427.4 11.7 %cholesky.164 = f32[128,128]{1,0:T(8,128)S(1)} custom-call(f32[128,128]{1,0:T(8,128)S(1)} %cholesky.197), custom_call_target="Cholesky" | custom-call | tf_op jit(solution)/shard_map/jit(cholesky)/cholesky | solution.py:70
  439.2 9.8 %custom-call.18 = f32[1,128,128]{1,2,0:T(8,128)S(1)} custom-call(f32[1,128,128]{2,1,0:T(8,128)S(1)} %get-tuple-element.44), custom_call_target="InvertDiagBlocksLowerTriangular" | custom-call | tf_op jit(solution)/shard_map/jit(cholesky)/cholesky | solution.py:70
  449.5 11.7 %cholesky.181 = f32[128,128]{1,0:T(8,128)S(1)} custom-call(f32[128,128]{1,0:T(8,128)S(1)} %convolution_subtract_fusion.2), custom_call_target="Cholesky" | custom-call | tf_op jit(solution)/shard_map/jit(cholesky)/cholesky | solution.py:70
  461.9 0.7 compare_reduce_fusion.1
  463.9 4.1 while.3
  463.9 0.7 fusion.47
  464.6 1.3 bitcast_dynamic-update-slice_fusion.5
  466.6 1.3 bitcast_dynamic-update-slice_fusion.5
  468.0 19.9 %custom-call.15 = f32[2,128,128]{1,2,0:T(8,128)S(1)} custom-call(f32[2,128,128]{2,1,0:T(8,128)S(1)} %get-tuple-element.18), custom_call_target="InvertDiagBlocksLowerTriangular" | custom-call | tf_op jit(solution)/shard_map/triangular_solve | solution.py:71
  487.9 1.8 fusion.25
  489.7 3.1 convolution_subtract_fusion
  492.8 1.8 convolution_convert_fusion
  494.6 1.1 pad_maximum_fusion
  (62 shorter events, 6.7 us)
Async XLA Ops:
  7.2 1.6 copy-start
  11.7 11.7 %all-to-all-start = ((f32[2,32,4,512]{3,2,1,0:T(4,128)}), f32[2,32,4,512]{3,2,1,0:T(4,128)S(1)}, u32[]{:S(2)}, u32[]{:S(2)}) async-start(f32[2,32,4,512]{3,2,1,0:T(4,128)} %bitcast.81), calls=%async_computation | async-start | bytes 1048576 | tf_op jit(solution)/shard_map/all_to_all | solution.py:17
  68.9 55.3 %all-to-all-start.4 = ((f32[8,256,256]{2,1,0:T(8,128)}), f32[8,256,256]{2,1,0:T(8,128)}, u32[]{:S(2)}, u32[]{:S(2)}) async-start(f32[8,256,256]{2,1,0:T(8,128)} %broadcast_in_dim.12), calls=%async_computation.4 | async-start | bytes 4194304 | tf_op jit(solution)/shard_map/all_to_all | solution.py:36
  75.8 279.1 %all-gather.3.cloned.1.call-start = ((), (), s32[]{:S(2)}) async-start(), calls=%async_computation.9 | async-start | bytes 18505728 | tf_op jit(solution)/shard_map/all_gather | solution.py:87
  187.4 2.1 copy-start.3
  374.4 113.5 %copy-start.2 = (f32[256,2004]{0,1:T(8,128)}, f32[256,2004]{0,1:T(8,128)S(1)}, u32[]{:S(2)}) copy-start(f32[256,2004]{0,1:T(8,128)S(1)} %bitcast_reduce_fusion) | copy-start | bytes 6156292
  489.7 6.0 %copy-start.1 = (bf16[512,2004]{0,1:T(8,128)(2,1)S(1)}, bf16[512,2004]{0,1:T(8,128)(2,1)}, u32[]{:S(2)}) copy-start(bf16[512,2004]{0,1:T(8,128)(2,1)} %param.3) | copy-start | bytes 6156292
Sparse Core Ops, SparseCore 0:
  189.6 165.2 all-gather.2
